TPU v7x, 512 devices: a whole 4x8x8 slice. The times are simulated.
512 devices in a mesh: tx: 16 (over z, core), ty: 8 (over y_hi, x), mode: 4 (over y_lo).
Axes of the slice: x: 4, y: 8 (y_hi: 2, y_lo: 4; y = y_hi * 4 + y_lo), z: 8, core: 2. Of those that a mesh axis runs over, the one named last changes fastest.
Arguments:
- object_field: float32 [2, 2048, 2048], P(None, 'tx', 'ty'), may hold values from -5 to 5
- probe: float32 [2, 8, 256, 256], P(None, 'mode'), may hold values from -1.5 to 1.5
- amplitudes: bfloat16 [16, 8, 2, 256, 256], P('tx', 'ty'), may hold values from 0.29882812 to 2.5
- centers: int32 [16, 8, 2, 2], P('tx', 'ty'), may hold values from 0 to 255, as said below
- live: int32 [16, 8], P('tx', 'ty'), may hold values from 1 to 2, as said below
Outputs:
- updated: float32 [2, 2048, 2048], P(None, 'tx', 'ty')
Inputs may be any that keep to these rules, and one draw needn't show every extreme that they name: `centers`: the first component is under 128, the second under 256; some live slot sits at offsets (127, 255) and some at (0, 0). A tile's positions fill its slots 0 to live - 1; some tile has all 2 slots live and some only one.
All inputs are finite; a program needn't handle non-finite values.
Results may differ from a plain program's by a relative error of at most 0.006.
Values may be sent and summed in bfloat16 or wider, within the bound.
A program may use at most 64 MiB of HBM per device.

v0:
```python
import math
import jax
import jax.numpy as jnp
from jax import lax
from jax.sharding import PartitionSpec as P

power_floor = 0.01
regularizer = 0.1


def padded_2(block, sides, width):
    for axis, dim in sides:
        count = lax.axis_size(axis)
        forward = [(i, i + 1) for i in range(count - 1)]
        backward = [(target, source) for source, target in forward]
        low = lax.ppermute(
            lax.slice_in_dim(block, block.shape[dim] - width, None, axis=dim), axis, forward
        )
        high = lax.ppermute(lax.slice_in_dim(block, 0, width, axis=dim), axis, backward)
        block = jnp.concatenate([low, block, high], axis=dim)
    return block


def dft_tables(pattern_side):
    index_line = jnp.arange(pattern_side, dtype=jnp.int32)
    product_table = index_line[:, None] * index_line[None, :] % pattern_side
    angle_table = product_table.astype(jnp.float32) * (2.0 * math.pi / pattern_side)
    scaling = 1.0 / math.sqrt(pattern_side)
    table_real = (jnp.cos(angle_table) * scaling).astype(jnp.bfloat16)
    table_imaginary = (-jnp.sin(angle_table) * scaling).astype(jnp.bfloat16)
    return (table_real, table_imaginary)


def left_mult(matrix, signal):
    return jnp.einsum("uv,kvw->kuw", matrix, signal, preferred_element_type=jnp.float32)


def right_mult(signal, matrix):
    return jnp.einsum("kuv,vw->kuw", signal, matrix, preferred_element_type=jnp.float32)


def left_apply(matrix_real, matrix_imaginary, signal_real, signal_imaginary):
    return (
        left_mult(matrix_real, signal_real) - left_mult(matrix_imaginary, signal_imaginary),
        left_mult(matrix_real, signal_imaginary) + left_mult(matrix_imaginary, signal_real),
    )


def right_apply(matrix_real, matrix_imaginary, signal_real, signal_imaginary):
    return (
        right_mult(signal_real, matrix_real) - right_mult(signal_imaginary, matrix_imaginary),
        right_mult(signal_real, matrix_imaginary) + right_mult(signal_imaginary, matrix_real),
    )


def forward_wave(patch, probe_real, probe_imaginary, table_real, table_imaginary):
    patch_real = patch[0].astype(jnp.float32)
    patch_imaginary = patch[1].astype(jnp.float32)
    exit_real = (probe_real * patch_real - probe_imaginary * patch_imaginary).astype(jnp.bfloat16)
    exit_imaginary = (probe_real * patch_imaginary + probe_imaginary * patch_real).astype(
        jnp.bfloat16
    )
    half_real, half_imaginary = left_apply(table_real, table_imaginary, exit_real, exit_imaginary)
    far_real, far_imaginary = right_apply(
        table_real,
        table_imaginary,
        half_real.astype(jnp.bfloat16),
        half_imaginary.astype(jnp.bfloat16),
    )
    return (exit_real, exit_imaginary, far_real, far_imaginary)


def backward_wave(
    far_real,
    far_imaginary,
    power,
    amplitude,
    exit_real,
    exit_imaginary,
    probe_real,
    probe_imaginary,
    table_real,
    table_imaginary,
):
    factor = amplitude.astype(jnp.float32) / jnp.sqrt(power + power_floor)
    fixed_real = (far_real * factor).astype(jnp.bfloat16)
    fixed_imaginary = (far_imaginary * factor).astype(jnp.bfloat16)
    back_half_real, back_half_imaginary = left_apply(
        table_real, -table_imaginary, fixed_real, fixed_imaginary
    )
    back_real, back_imaginary = right_apply(
        table_real,
        -table_imaginary,
        back_half_real.astype(jnp.bfloat16),
        back_half_imaginary.astype(jnp.bfloat16),
    )
    diff_real = back_real - exit_real.astype(jnp.float32)
    diff_imaginary = back_imaginary - exit_imaginary.astype(jnp.float32)
    grad_real = jnp.sum(probe_real * diff_real + probe_imaginary * diff_imaginary, axis=0)
    grad_imaginary = jnp.sum(probe_real * diff_imaginary - probe_imaginary * diff_real, axis=0)
    return (grad_real, grad_imaginary)


def on_device(object_field, probe, amplitudes, centers, live):
    pattern_side = probe.shape[2]
    half_width = pattern_side // 2
    tile_rows = object_field.shape[1]
    tile_cols = object_field.shape[2]
    slot_total = centers.shape[2]
    channels = 3
    table_real, table_imaginary = dft_tables(pattern_side)
    object_low = object_field.astype(jnp.bfloat16)
    padded = padded_2(object_low, (("tx", 1), ("ty", 2)), half_width)
    live_count = live[0, 0]
    anchor = jnp.zeros((), jnp.int32)
    extended = jnp.zeros(
        (channels, tile_rows + pattern_side, tile_cols + pattern_side), jnp.float32
    )

    def place_of(slot_index):
        return (centers[0, 0, slot_index, 0], centers[0, 0, slot_index, 1])

    def patch_of(row_at, col_at):
        return lax.dynamic_slice(padded, (anchor, row_at, col_at), (2, pattern_side, pattern_side))

    def deposit(extended, row_at, col_at, grad_real, grad_imaginary, weight):
        block = jnp.stack([grad_real, grad_imaginary, weight])
        current = lax.dynamic_slice(
            extended, (anchor, row_at, col_at), (channels, pattern_side, pattern_side)
        )
        return lax.dynamic_update_slice(extended, current + block, (anchor, row_at, col_at))

    probe_real = probe[0]
    probe_imaginary = probe[1]
    modes_here = probe.shape[1]
    weight = jnp.sum(probe_real * probe_real + probe_imaginary * probe_imaginary, axis=0)
    far_store = jnp.zeros((slot_total, 2, modes_here, pattern_side, pattern_side), jnp.float32)
    exit_store = jnp.zeros((slot_total, 2, modes_here, pattern_side, pattern_side), jnp.bfloat16)
    power_part = jnp.zeros((slot_total, pattern_side, pattern_side), jnp.float32)

    def look(slot_index, state):
        far_store, exit_store, power_part = state
        row_at, col_at = place_of(slot_index)
        exit_real, exit_imaginary, far_real, far_imaginary = forward_wave(
            patch_of(row_at, col_at), probe_real, probe_imaginary, table_real, table_imaginary
        )
        far_store = lax.dynamic_update_index_in_dim(
            far_store, jnp.stack([far_real, far_imaginary]), slot_index, 0
        )
        exit_store = lax.dynamic_update_index_in_dim(
            exit_store, jnp.stack([exit_real, exit_imaginary]), slot_index, 0
        )
        power_slot = jnp.sum(far_real * far_real + far_imaginary * far_imaginary, axis=0)
        power_part = lax.dynamic_update_index_in_dim(power_part, power_slot, slot_index, 0)
        return (far_store, exit_store, power_part)

    far_store, exit_store, power_part = lax.fori_loop(
        0, live_count, look, (far_store, exit_store, power_part)
    )
    power_all = lax.psum(power_part.astype(jnp.bfloat16), "mode").astype(jnp.float32)

    def apply_slot(slot_index, extended):
        row_at, col_at = place_of(slot_index)
        far_slot = lax.dynamic_index_in_dim(far_store, slot_index, 0, keepdims=False)
        exit_slot = lax.dynamic_index_in_dim(exit_store, slot_index, 0, keepdims=False)
        power = lax.dynamic_index_in_dim(power_all, slot_index, 0, keepdims=False)
        amplitude = lax.dynamic_index_in_dim(amplitudes[0, 0], slot_index, 0, keepdims=False)
        grad_real, grad_imaginary = backward_wave(
            far_slot[0],
            far_slot[1],
            power,
            amplitude,
            exit_slot[0],
            exit_slot[1],
            probe_real,
            probe_imaginary,
            table_real,
            table_imaginary,
        )
        return deposit(extended, row_at, col_at, grad_real, grad_imaginary, weight)

    extended = lax.fori_loop(0, live_count, apply_slot, extended)
    rows_out = jnp.concatenate(
        [extended[:, :half_width, :], extended[:, tile_rows + half_width :, :]], axis=1
    )
    rows_back = padded_2(rows_out.astype(jnp.bfloat16), (("tx", 1),), half_width).astype(
        rows_out.dtype
    )
    inner = extended[:, half_width : half_width + tile_rows, :]
    inner = inner.at[:, :half_width, :].add(rows_back[:, :half_width, :])
    inner = inner.at[:, tile_rows - half_width :, :].add(rows_back[:, 3 * half_width :, :])
    cols_out = jnp.concatenate(
        [inner[:, :, :half_width], inner[:, :, tile_cols + half_width :]], axis=2
    )
    cols_back = padded_2(cols_out.astype(jnp.bfloat16), (("ty", 2),), half_width).astype(
        cols_out.dtype
    )
    core = inner[:, :, half_width : half_width + tile_cols]
    core = core.at[:, :, :half_width].add(cols_back[:, :, :half_width])
    core = core.at[:, :, tile_cols - half_width :].add(cols_back[:, :, 3 * half_width :])
    summed = lax.psum(core.astype(jnp.bfloat16), "mode").astype(jnp.float32)
    return object_field + summed[:2] / (summed[2] + regularizer)


def solution(mesh):
    return jax.shard_map(
        on_device,
        mesh=mesh,
        in_specs=(
            P(None, "tx", "ty"),
            P(None, "mode", None, None),
            P("tx", "ty", None, None, None),
            P("tx", "ty", None, None),
            P("tx", "ty"),
        ),
        out_specs=P(None, "tx", "ty"),
        check_vma=False,
    )
```

profile of v0, /device:TPU:2, one launch (start us, length us, event | category | flops | bytes accessed | tf_op | source)
XLA Modules:
  0.0 308.4 jit_solution(16685017725092557172)
XLA Ops:
  9.0 3.0 collective-permute-start
  13.1 3.4 %collective-permute-start.2 = (bf16[2,384,128]{1,2,0:T(8,128)(2,1)S(1)}, bf16[2,384,128]{1,2,0:T(8,128)(2,1)S(1)}, u32[]{:S(2)}, u32[]{:S(2)}) collective-permute-start(bf16[2,384,128]{1,2,0:T(8,128)(2,1)S(1)} %get-tuple-element.527), channel_id=1, source_target_pairs={{0,4},{4,8},{8,12},{12,16},{16,20},{20,24},{24,28},{1,5},{5,9},{9,... | collective-permute-start | bytes 589832 | tf_op jit(solution)/shard_map/ppermute | solution.py:16
  16.5 5.7 %collective-permute-start.3 = (bf16[2,384,128]{1,2,0:T(8,128)(2,1)S(1)}, bf16[2,384,128]{1,2,0:T(8,128)(2,1)}, u32[]{:S(2)}, u32[]{:S(2)}) collective-permute-start(bf16[2,384,128]{1,2,0:T(8,128)(2,1)S(1)} %get-tuple-element.528), channel_id=1, source_target_pairs={{4,0},{8,4},{12,8},{16,12},{20,16},{24,20},{28,24},{5,1},{9,5},{13... | collective-permute-start | bytes 589832 | tf_op jit(solution)/shard_map/ppermute | solution.py:19
  23.3 2.4 collective-permute-done.2
  31.9 39.6 %while.36 = (s32[]{:T(128)}, f32[2,2,2,256,256]{4,3,2,1,0:T(8,128)}, bf16[2,2,2,256,256]{3,4,2,1,0:T(8,128)(2,1)}, bf16[2,256,256]{1,2,0:T(8,128)(2,1)}, s32[]{:...) while((s32[]{:T(128)}, ...), condition=%wide.region_2.3_spmd.clone.clone, body=%wide.region_0.2_spmd.clone.clone.sunk | while | flops 550305792 | bytes 17170740 | solution.py:157
  46.0 1.9 add_reduce_fusion.5
  65.5 1.9 add_reduce_fusion.5
  71.6 2.0 add_reduce_fusion.2
  73.6 66.5 %all-reduce.3.cloned.1.call-done = bf16[2,256,256]{1,2,0:T(8,128)(2,1)} async-done(((bf16[2,256,256]{1,2,0:T(8,128)(2,1)}), bf16[2,256,256]{1,2,0:T(8,128)(2,1)}) %all-reduce.3.cloned.1.call-update) | async-done | bytes 262160 | tf_op jit(solution)/shard_map/psum | solution.py:160
  140.2 1.8 convert_element_type.192
  142.3 78.2 %while.37 = (s32[]{:T(128)}, f32[3,384,512]{2,1,0:T(8,128)S(1)}, s32[]{:T(128)}, s32[1,1,2,2]{3,2,1,0:T(2,128)S(1)}, f32[2,2,2,256,256]{4,3,2,1,0:T(8,128)}, /*i...) while((s32[]{:T(128)}, f32[3,384,512]{2,1,0:T(8,128)S(1)}, ...), condition=%wide.region_8.9_spmd.clone.clone, body=%wide.region_5.8_spmd.clone.clone.sunk | while | flops 550371328 | bytes 32899572 | solution.py:182
  148.6 1.7 fusion.264
  155.5 2.2 fusion.268
  157.7 2.3 fusion.269
  168.7 13.0 %dynamic_update_slice.35 = f32[3,384,512]{2,1,0:T(8,128)S(1)} dynamic-update-slice(f32[3,384,512]{2,1,0:T(8,128)S(1)} %get-tuple-element.752, f32[3,256,256]{2,1,0:T(8,128)S(1)} %maximum_add_fusion.2, s32[]{:T(128)} %constant.211.clone.1..sunk.1, s32[]{:T(128)S(6)} %select_n.188, s32[]{:T(128)S(6)} %select_n.189) | dynamic-update-slice | bytes 1572868 | tf_op jit(solution)/shard_map/while/body/dynamic_update_slice | solution.py:131
  187.8 1.7 fusion.264
  194.8 2.2 fusion.268
  197.0 2.3 fusion.269
  207.9 12.0 %dynamic_update_slice.35 = f32[3,384,512]{2,1,0:T(8,128)S(1)} dynamic-update-slice(f32[3,384,512]{2,1,0:T(8,128)S(1)} %get-tuple-element.752, f32[3,256,256]{2,1,0:T(8,128)S(1)} %maximum_add_fusion.2, s32[]{:T(128)} %constant.211.clone.1..sunk.1, s32[]{:T(128)S(6)} %select_n.188, s32[]{:T(128)S(6)} %select_n.189) | dynamic-update-slice | bytes 1572868 | tf_op jit(solution)/shard_map/while/body/dynamic_update_slice | solution.py:131
  223.3 2.3 collective-permute-done.5
  225.9 2.1 collective-permute-start.6
  227.9 3.9 %collective-permute-start.7 = (bf16[3,128,128]{2,1,0:T(8,128)(2,1)S(1)}, bf16[3,128,128]{2,1,0:T(8,128)(2,1)S(1)}, u32[]{:S(2)}, u32[]{:S(2)}) collective-permute-start(bf16[3,128,128]{2,1,0:T(8,128)(2,1)S(1)} %get-tuple-element.526), channel_id=1, source_target_pairs={{4,0},{8,4},{12,8},{16,12},{20,16},{24,20},{28,24},{5,1},{9,5},{13... | collective-permute-start | bytes 294920 | tf_op jit(solution)/shard_map/ppermute | solution.py:19
  232.5 1.9 collective-permute-done.7
  235.3 64.6 %all-reduce.5.cloned.1.call-done = bf16[3,128,256]{2,1,0:T(8,128)(2,1)} async-done(((bf16[3,128,256]{2,1,0:T(8,128)(2,1)}), bf16[3,128,256]{2,1,0:T(8,128)(2,1)}) %all-reduce.5.cloned.1.call-update) | async-done | bytes 196624 | tf_op jit(solution)/shard_map/psum | solution.py:201
  (140 shorter events, 73.7 us)
Async XLA Ops:
  6.5 15.7 %copy-start.8 = (f32[2,2,256,256]{3,2,1,0:T(8,128)S(1)}, f32[2,2,256,256]{3,2,1,0:T(8,128)}, u32[]{:S(2)}) copy-start(f32[2,2,256,256]{3,2,1,0:T(8,128)} %param.22) | copy-start | bytes 3145732
  6.5 133.6 %all-reduce.3.cloned.1.call-start = ((), (), s32[]{:S(2)}) async-start(), calls=%async_computation | async-start | bytes 524288 | tf_op jit(solution)/shard_map/psum | solution.py:160
  7.7 4.3 %collective-permute-start.1 = (bf16[2,128,256]{1,2,0:T(8,128)(2,1)S(1)}, bf16[2,128,256]{1,2,0:T(8,128)(2,1)S(1)}, u32[]{:S(2)}, u32[]{:S(2)}) collective-permute-start(bf16[2,128,256]{1,2,0:T(8,128)(2,1)S(1)} %copy.14), channel_id=1, source_target_pairs={{32,0},{64,32},{96,64},{128,96},{160,128},{192,160},{224,192},{256... | collective-permute-start | bytes 393224 | tf_op jit(solution)/shard_map/ppermute | solution.py:19
  9.0 4.0 %collective-permute-start = (bf16[2,128,256]{1,2,0:T(8,128)(2,1)S(1)}, bf16[2,128,256]{1,2,0:T(8,128)(2,1)S(1)}, u32[]{:S(2)}, u32[]{:S(2)}) collective-permute-start(bf16[2,128,256]{1,2,0:T(8,128)(2,1)S(1)} %copy.14), channel_id=1, source_target_pairs={{0,32},{32,64},{64,96},{96,128},{128,160},{160,192},{192,224},{224... | collective-permute-start | bytes 393224 | tf_op jit(solution)/shard_map/ppermute | solution.py:16
  12.1 10.3 %copy-start.10 = (bf16[2,128,256]{1,2,0:T(8,128)(2,1)}, bf16[2,128,256]{1,2,0:T(8,128)(2,1)S(1)}, u32[]{:S(2)}) copy-start(bf16[2,128,256]{1,2,0:T(8,128)(2,1)S(1)} %collective-permute-done.1) | copy-start | bytes 393220
  13.0 9.3 %copy-start.12 = (bf16[2,128,256]{1,2,0:T(8,128)(2,1)}, bf16[2,128,256]{1,2,0:T(8,128)(2,1)S(1)}, u32[]{:S(2)}) copy-start(bf16[2,128,256]{1,2,0:T(8,128)(2,1)S(1)} %collective-permute-done) | copy-start | bytes 393220
  13.1 12.6 %collective-permute-start.2 = (bf16[2,384,128]{1,2,0:T(8,128)(2,1)S(1)}, bf16[2,384,128]{1,2,0:T(8,128)(2,1)S(1)}, u32[]{:S(2)}, u32[]{:S(2)}) collective-permute-start(bf16[2,384,128]{1,2,0:T(8,128)(2,1)S(1)} %get-tuple-element.527), channel_id=1, source_target_pairs={{0,4},{4,8},{8,12},{12,16},{16,20},{20,24},{24,28},{1,5},{5,9},{9,... | collective-permute-start | bytes 589832 | tf_op jit(solution)/shard_map/ppermute | solution.py:16
  16.5 11.0 %collective-permute-start.3 = (bf16[2,384,128]{1,2,0:T(8,128)(2,1)S(1)}, bf16[2,384,128]{1,2,0:T(8,128)(2,1)}, u32[]{:S(2)}, u32[]{:S(2)}) collective-permute-start(bf16[2,384,128]{1,2,0:T(8,128)(2,1)S(1)} %get-tuple-element.528), channel_id=1, source_target_pairs={{4,0},{8,4},{12,8},{16,12},{20,16},{24,20},{28,24},{5,1},{9,5},{13... | collective-permute-start | bytes 589832 | tf_op jit(solution)/shard_map/ppermute | solution.py:19
  22.4 8.1 %copy-start.3 = (f32[2,256,256]{2,1,0:T(8,128)}, f32[2,256,256]{2,1,0:T(8,128)S(1)}, u32[]{:S(2)}) copy-start(f32[2,256,256]{2,1,0:T(8,128)S(1)} %get-tuple-element.742) | copy-start | bytes 1572868
  22.4 5.1 %copy-start.11 = (bf16[2,128,256]{1,2,0:T(8,128)(2,1)S(1)}, bf16[2,128,256]{1,2,0:T(8,128)(2,1)}, u32[]{:S(2)}) copy-start(bf16[2,128,256]{1,2,0:T(8,128)(2,1)} %copy-done.10) | copy-start | bytes 393220
  22.4 5.1 %copy-start.13 = (bf16[2,128,256]{1,2,0:T(8,128)(2,1)S(1)}, bf16[2,128,256]{1,2,0:T(8,128)(2,1)}, u32[]{:S(2)}) copy-start(bf16[2,128,256]{1,2,0:T(8,128)(2,1)} %copy-done.12) | copy-start | bytes 393220
  28.6 3.3 %copy-start.15 = (s32[1,1,2,2]{3,2,1,0:T(2,128)S(1)}, s32[1,1,2,2]{3,2,1,0:T(2,128)}, u32[]{:S(2)}) copy-start(s32[1,1,2,2]{3,2,1,0:T(2,128)} %param.24) | copy-start | bytes 52
  71.6 228.3 %all-reduce.5.cloned.1.call-start = ((), (), s32[]{:S(2)}) async-start(), calls=%async_computation.1 | async-start | bytes 393216 | tf_op jit(solution)/shard_map/psum | solution.py:201
  155.5 4.5 %copy-start.5 = (f32[1,1,2,256,256]{3,4,2,1,0:T(8,128)S(1)}, f32[1,1,2,256,256]{3,4,2,1,0:T(8,128)}, u32[]{:S(2)}) copy-start(f32[1,1,2,256,256]{3,4,2,1,0:T(8,128)} %copy.46) | copy-start | bytes 1572868 | tf_op jit(solution)/shard_map/while
  155.5 4.5 %copy-start.7 = (f32[256,256]{0,1:T(8,128)S(1)}, f32[256,256]{0,1:T(8,128)}, u32[]{:S(2)}) copy-start(f32[256,256]{0,1:T(8,128)} %fusion.264) | copy-start | bytes 786436 | tf_op jit(solution)/shard_map/while
  161.2 3.6 %copy-start.6 = (bf16[1,1,2,256,256]{4,3,2,1,0:T(8,128)(2,1)S(1)}, bf16[1,1,2,256,256]{4,3,2,1,0:T(8,128)(2,1)}, u32[]{:S(2)}) copy-start(bf16[1,1,2,256,256]{4,3,2,1,0:T(8,128)(2,1)} %copy.49) | copy-start | bytes 786436 | tf_op jit(solution)/shard_map/while
  194.7 4.5 %copy-start.5 = (f32[1,1,2,256,256]{3,4,2,1,0:T(8,128)S(1)}, f32[1,1,2,256,256]{3,4,2,1,0:T(8,128)}, u32[]{:S(2)}) copy-start(f32[1,1,2,256,256]{3,4,2,1,0:T(8,128)} %copy.46) | copy-start | bytes 1572868 | tf_op jit(solution)/shard_map/while
  194.8 4.5 %copy-start.7 = (f32[256,256]{0,1:T(8,128)S(1)}, f32[256,256]{0,1:T(8,128)}, u32[]{:S(2)}) copy-start(f32[256,256]{0,1:T(8,128)} %fusion.264) | copy-start | bytes 786436 | tf_op jit(solution)/shard_map/while
  200.5 3.6 %copy-start.6 = (bf16[1,1,2,256,256]{4,3,2,1,0:T(8,128)(2,1)S(1)}, bf16[1,1,2,256,256]{4,3,2,1,0:T(8,128)(2,1)}, u32[]{:S(2)}) copy-start(bf16[1,1,2,256,256]{4,3,2,1,0:T(8,128)(2,1)} %copy.49) | copy-start | bytes 786436 | tf_op jit(solution)/shard_map/while
  220.7 2.6 collective-permute-start.4
  222.0 3.6 %collective-permute-start.5 = (bf16[3,128,512]{2,1,0:T(8,128)(2,1)S(1)}, bf16[3,128,512]{2,1,0:T(8,128)(2,1)S(1)}, u32[]{:S(2)}, u32[]{:S(2)}) collective-permute-start(bf16[3,128,512]{2,1,0:T(8,128)(2,1)S(1)} %get-tuple-element.522), channel_id=1, source_target_pairs={{32,0},{64,32},{96,64},{128,96},{160,128},{192,160},{224,192},{256... | collective-permute-start | bytes 1179656 | tf_op jit(solution)/shard_map/ppermute | solution.py:19
  225.9 75.0 %copy-start.9 = (f32[2,128,256]{2,1,0:T(8,128)S(1)}, f32[2,128,256]{2,1,0:T(8,128)}, u32[]{:S(2)}) copy-start(f32[2,128,256]{2,1,0:T(8,128)} %param.21) | copy-start | bytes 786436
  225.9 6.6 %collective-permute-start.6 = (bf16[3,128,128]{2,1,0:T(8,128)(2,1)S(1)}, bf16[3,128,128]{2,1,0:T(8,128)(2,1)S(1)}, u32[]{:S(2)}, u32[]{:S(2)}) collective-permute-start(bf16[3,128,128]{2,1,0:T(8,128)(2,1)S(1)} %get-tuple-element.525), channel_id=1, source_target_pairs={{0,4},{4,8},{8,12},{12,16},{16,20},{20,24},{24,28},{1,5},{5,9},{9,... | collective-permute-start | bytes 294920 | tf_op jit(solution)/shard_map/ppermute | solution.py:16
  227.9 6.5 %collective-permute-start.7 = (bf16[3,128,128]{2,1,0:T(8,128)(2,1)S(1)}, bf16[3,128,128]{2,1,0:T(8,128)(2,1)S(1)}, u32[]{:S(2)}, u32[]{:S(2)}) collective-permute-start(bf16[3,128,128]{2,1,0:T(8,128)(2,1)S(1)} %get-tuple-element.526), channel_id=1, source_target_pairs={{4,0},{8,4},{12,8},{16,12},{20,16},{24,20},{28,24},{5,1},{9,5},{13... | collective-permute-start | bytes 294920 | tf_op jit(solution)/shard_map/ppermute | solution.py:19
  (8 other events, 16.0 us)
Sparse Core Ops, SparseCore 0:
  71.7 68.4 all-reduce.2
  235.4 64.4 all-reduce.4
where the time goes:
time: 310 us; the launch traced here: 308 us
  waiting for transfers between devices  140 us (45%)
  local copies, waits for them, and re-layouts  49.8 us (16%)
  matrix products  43.8 us (14%)
  starting transfers between devices  22 us (7%)
  loops' own time  20.2 us (7%)
  other arithmetic  18.4 us (6%)
  between operations  13.7 us (4%)
    psum x1, waiting for transfers between devices, on_device(): lax.psum(power_part.astype(jnp.bfloat16), 'mode').astype(jnp.float32)  66.5 us
    psum x1, waiting for transfers between devices, on_device(): summed = lax.psum(core.astype(jnp.bfloat16), 'mode').astype(jnp.float32)  64.6 us
    dynamic_update_slice x2, local copies, waits for them, and re-layouts, deposit(): lax.dynamic_update_slice(extended, current + block, (anchor, row_at, col_...  25 us
    dot_general x16, matrix products, left_mult(): jnp.einsum('uv,kvw->kuw', matrix, signal, preferred_element_type=jnp.floa...  23.1 us
    dot_general x16, matrix products, right_mult(): jnp.einsum('kuv,vw->kuw', signal, matrix, preferred_element_type=jnp.floa...  20.7 us
    ppermute x4, starting transfers between devices, padded_2(): lax.ppermute(lax.slice_in_dim(block, 0, width, axis=dim), axis, backward)  12.2 us
    another operation x1, loops' own time, on_device(): extended = lax.fori_loop(0, live_count, apply_slot, extended)  10.2 us
    another operation x1, loops' own time, on_device(): lax.fori_loop(0, live_count, look, (far_store, exit_store, power_part))  10 us
  transfers between devices with their start and end apart: 10, of which 8 were waited for; matrix products, arithmetic and copies ran while one was open for 1% of the time, Pallas kernels for 0%

commit v1 on v0

--- a/solution.py
+++ b/solution.py
@@ -198,7 +198,13 @@
     core = inner[:, :, half_width : half_width + tile_cols]
     core = core.at[:, :, :half_width].add(cols_back[:, :, :half_width])
     core = core.at[:, :, tile_cols - half_width :].add(cols_back[:, :, 3 * half_width :])
-    summed = lax.psum(core.astype(jnp.bfloat16), "mode").astype(jnp.float32)
+
+    def _reach_run(mine):
+        y2 = lax.all_gather(mine, axis_name="mode")
+        v1 = jnp.sum(y2, 0)
+        return v1
+
+    summed = _reach_run(core.astype(jnp.bfloat16)).astype(jnp.float32)
     return object_field + summed[:2] / (summed[2] + regularizer)
 
 

time: 310 us -> 274 us (0.88)
  the two profiles are of different devices: /device:TPU:2 before, /device:TPU:198 now
where the time goes in v1:
time: 274 us; the launch traced here: 273 us
  waiting for transfers between devices  139 us (51%)
  starting transfers between devices  27.7 us (10%)
  local copies, waits for them, and re-layouts  27.2 us (10%)
  matrix products  21.9 us (8%)
  blocking collectives  21 us (8%)
  between operations  13.7 us (5%)
  other arithmetic  11.6 us (4%)
  loops' own time  10.8 us (4%)
    psum x1, waiting for transfers between devices, on_device(): lax.psum(power_part.astype(jnp.bfloat16), 'mode').astype(jnp.float32)  71.6 us
    ppermute x4, waiting for transfers between devices, padded_2(): lax.ppermute(lax.slice_in_dim(block, 0, width, axis=dim), axis, backward)  58.2 us
    all_gather x1, blocking collectives, _reach_run(): y2 = lax.all_gather(mine, axis_name='mode')  21 us
    ppermute x4, starting transfers between devices, padded_2(): lax.ppermute(lax.slice_in_dim(block, block.shape[dim] - width, None, axis...  18.3 us
    dot_general x8, matrix products, left_mult(): jnp.einsum('uv,kvw->kuw', matrix, signal, preferred_element_type=jnp.floa...  11.6 us
    dynamic_update_slice x1, local copies, waits for them, and re-layouts, deposit(): lax.dynamic_update_slice(extended, current + block, (anchor, row_at, col_...  11.5 us
    dot_general x8, matrix products, right_mult(): jnp.einsum('kuv,vw->kuw', signal, matrix, preferred_element_type=jnp.floa...  10.3 us
    ppermute x4, waiting for transfers between devices, padded_2(): lax.ppermute(lax.slice_in_dim(block, block.shape[dim] - width, None, axis...  9.48 us
  transfers between devices with their start and end apart: 9, of which 9 were waited for; matrix products, arithmetic and copies ran while one was open for 1% of the time, Pallas kernels for 0%

profile of v1, /device:TPU:198, one launch (start us, length us, event | category | flops | bytes accessed | tf_op | source)
XLA Modules:
  0.0 273.1 jit_solution(16836496967743407958)
XLA Ops:
  7.7 1.9 collective-permute-start.1
  9.6 2.4 collective-permute-start
  12.1 3.8 %collective-permute-done = bf16[2,128,256]{1,2,0:T(8,128)(2,1)S(1)} collective-permute-done((bf16[2,128,256]{1,2,0:T(8,128)(2,1)S(1)}, bf16[2,128,256]{1,2,0:T(8,128)(2,1)S(1)}, u32[]{:S(2)}, u32[]{:S(2)}) %collective-permute-start) | collective-permute-done | bytes 131104 | tf_op jit(solution)/shard_map/ppermute | solution.py:16
  16.0 7.6 %collective-permute-start.2 = (bf16[2,384,128]{1,2,0:T(8,128)(2,1)S(1)}, bf16[2,384,128]{1,2,0:T(8,128)(2,1)S(1)}, u32[]{:S(2)}, u32[]{:S(2)}) collective-permute-start(bf16[2,384,128]{1,2,0:T(8,128)(2,1)S(1)} %get-tuple-element.547), channel_id=1, source_target_pairs={{0,4},{4,8},{8,12},{12,16},{16,20},{20,24},{24,28},{1,5},{5,9},{9,... | collective-permute-start | bytes 589832 | tf_op jit(solution)/shard_map/ppermute | solution.py:16
  23.7 1.9 collective-permute-start.3
  26.7 2.0 collective-permute-done.2
  29.3 10.2 %collective-permute-done.3 = bf16[2,384,128]{1,2,0:T(8,128)(2,1)} collective-permute-done((bf16[2,384,128]{1,2,0:T(8,128)(2,1)S(1)}, bf16[2,384,128]{1,2,0:T(8,128)(2,1)}, u32[]{:S(2)}, u32[]{:S(2)}) %collective-permute-start.3) | collective-permute-done | bytes 196640 | tf_op jit(solution)/shard_map/ppermute | solution.py:19
  44.0 19.9 %while.36 = (s32[]{:T(128)}, f32[2,2,2,256,256]{4,3,2,1,0:T(8,128)}, bf16[2,2,2,256,256]{3,4,2,1,0:T(8,128)(2,1)}, bf16[2,256,256]{1,2,0:T(8,128)(2,1)}, s32[]{:...) while((s32[]{:T(128)}, ...), condition=%wide.region_2.3_spmd.clone.clone, body=%wide.region_0.2_spmd.clone.clone.sunk | while | flops 550305792 | bytes 17170740 | solution.py:157
  57.8 1.9 add_reduce_fusion.5
  64.0 2.0 add_reduce_fusion.2
  66.0 71.6 %all-reduce.2.cloned.1.call-done = bf16[2,256,256]{1,2,0:T(8,128)(2,1)} async-done(((bf16[2,256,256]{1,2,0:T(8,128)(2,1)}), bf16[2,256,256]{1,2,0:T(8,128)(2,1)}) %all-reduce.2.cloned.1.call-update) | async-done | bytes 262160 | tf_op jit(solution)/shard_map/psum | solution.py:160
  137.6 1.8 convert_element_type.194
  139.6 38.7 %while.37 = (s32[]{:T(128)}, f32[3,384,512]{2,1,0:T(8,128)S(1)}, s32[]{:T(128)}, s32[1,1,2,2]{3,2,1,0:T(2,128)S(1)}, f32[2,2,2,256,256]{4,3,2,1,0:T(8,128)}, /*i...) while((s32[]{:T(128)}, f32[3,384,512]{2,1,0:T(8,128)S(1)}, ...), condition=%wide.region_8.9_spmd.clone.clone, body=%wide.region_5.8_spmd.clone.clone.sunk | while | flops 550371328 | bytes 32899572 | solution.py:182
  153.0 2.2 fusion.268
  155.2 2.3 fusion.269
  166.1 11.5 %dynamic_update_slice.35 = f32[3,384,512]{2,1,0:T(8,128)S(1)} dynamic-update-slice(f32[3,384,512]{2,1,0:T(8,128)S(1)} %get-tuple-element.772, f32[3,256,256]{2,1,0:T(8,128)S(1)} %maximum_add_fusion.2, s32[]{:T(128)} %constant.212.clone.1..sunk.1, s32[]{:T(128)S(6)} %select_n.188, s32[]{:T(128)S(6)} %select_n.189) | dynamic-update-slice | bytes 1572868 | tf_op jit(solution)/shard_map/while/body/dynamic_update_slice | solution.py:131
  178.5 1.9 collective-permute-start.4
  180.4 3.6 %collective-permute-start.5 = (bf16[3,128,512]{2,1,0:T(8,128)(2,1)S(1)}, bf16[3,128,512]{2,1,0:T(8,128)(2,1)S(1)}, u32[]{:S(2)}, u32[]{:S(2)}) collective-permute-start(bf16[3,128,512]{2,1,0:T(8,128)(2,1)S(1)} %get-tuple-element.542), channel_id=1, source_target_pairs={{32,0},{64,32},{96,64},{128,96},{160,128},{192,160},{224,192},{256... | collective-permute-start | bytes 1179656 | tf_op jit(solution)/shard_map/ppermute | solution.py:19
  184.1 3.5 %collective-permute-done.4 = bf16[3,128,512]{2,1,0:T(8,128)(2,1)S(1)} collective-permute-done((bf16[3,128,512]{2,1,0:T(8,128)(2,1)S(1)}, bf16[3,128,512]{2,1,0:T(8,128)(2,1)S(1)}, u32[]{:S(2)}, u32[]{:S(2)}) %collective-permute-start.4) | collective-permute-done | bytes 393248 | tf_op jit(solution)/shard_map/ppermute | solution.py:16
  187.6 37.6 %collective-permute-done.5 = bf16[3,128,512]{2,1,0:T(8,128)(2,1)S(1)} collective-permute-done((bf16[3,128,512]{2,1,0:T(8,128)(2,1)S(1)}, bf16[3,128,512]{2,1,0:T(8,128)(2,1)S(1)}, u32[]{:S(2)}, u32[]{:S(2)}) %collective-permute-start.5) | collective-permute-done | bytes 393248 | tf_op jit(solution)/shard_map/ppermute | solution.py:19
  225.4 6.3 %collective-permute-start.6 = (bf16[3,128,128]{2,1,0:T(8,128)(2,1)S(1)}, bf16[3,128,128]{2,1,0:T(8,128)(2,1)S(1)}, u32[]{:S(2)}, u32[]{:S(2)}) collective-permute-start(bf16[3,128,128]{2,1,0:T(8,128)(2,1)S(1)} %get-tuple-element.545), channel_id=1, source_target_pairs={{0,4},{4,8},{8,12},{12,16},{16,20},{20,24},{24,28},{1,5},{5,9},{9,... | collective-permute-start | bytes 294920 | tf_op jit(solution)/shard_map/ppermute | solution.py:16
  231.7 1.9 collective-permute-start.7
  233.9 10.4 %collective-permute-done.7 = bf16[3,128,128]{2,1,0:T(8,128)(2,1)S(1)} collective-permute-done((bf16[3,128,128]{2,1,0:T(8,128)(2,1)S(1)}, bf16[3,128,128]{2,1,0:T(8,128)(2,1)S(1)}, u32[]{:S(2)}, u32[]{:S(2)}) %collective-permute-start.7) | collective-permute-done | bytes 98336 | tf_op jit(solution)/shard_map/ppermute | solution.py:19
  244.4 21.0 %all-gather = bf16[12,128,256]{2,1,0:T(8,128)(2,1)S(1)} all-gather(bf16[3,128,256]{2,1,0:T(8,128)(2,1)S(1)} %convert_element_type.197), channel_id=2, replica_groups=mesh['tx'=16,'ty'=8,'mode'=4] {'mode'}, dimensions={0}, use_global_device_ids=true | all-gather | bytes 983040 | tf_op jit(solution)/shard_map/all_gather | solution.py:203
  (91 shorter events, 39.4 us)
Async XLA Ops:
  6.5 19.1 %copy-start.8 = (f32[2,2,256,256]{3,2,1,0:T(8,128)S(1)}, f32[2,2,256,256]{3,2,1,0:T(8,128)}, u32[]{:S(2)}) copy-start(f32[2,2,256,256]{3,2,1,0:T(8,128)} %param.22) | copy-start | bytes 3145732
  6.5 131.0 %all-reduce.2.cloned.1.call-start = ((), (), s32[]{:S(2)}) async-start(), calls=%async_computation | async-start | bytes 524288 | tf_op jit(solution)/shard_map/psum | solution.py:160
  7.7 4.4 %collective-permute-start.1 = (bf16[2,128,256]{1,2,0:T(8,128)(2,1)S(1)}, bf16[2,128,256]{1,2,0:T(8,128)(2,1)S(1)}, u32[]{:S(2)}, u32[]{:S(2)}) collective-permute-start(bf16[2,128,256]{1,2,0:T(8,128)(2,1)S(1)} %copy.29), channel_id=1, source_target_pairs={{32,0},{64,32},{96,64},{128,96},{160,128},{192,160},{224,192},{256... | collective-permute-start | bytes 393224 | tf_op jit(solution)/shard_map/ppermute | solution.py:19
  9.6 6.3 %collective-permute-start = (bf16[2,128,256]{1,2,0:T(8,128)(2,1)S(1)}, bf16[2,128,256]{1,2,0:T(8,128)(2,1)S(1)}, u32[]{:S(2)}, u32[]{:S(2)}) collective-permute-start(bf16[2,128,256]{1,2,0:T(8,128)(2,1)S(1)} %copy.29), channel_id=1, source_target_pairs={{0,32},{32,64},{64,96},{96,128},{128,160},{160,192},{192,224},{224... | collective-permute-start | bytes 393224 | tf_op jit(solution)/shard_map/ppermute | solution.py:16
  12.1 13.6 %copy-start.10 = (bf16[2,128,256]{1,2,0:T(8,128)(2,1)}, bf16[2,128,256]{1,2,0:T(8,128)(2,1)S(1)}, u32[]{:S(2)}) copy-start(bf16[2,128,256]{1,2,0:T(8,128)(2,1)S(1)} %collective-permute-done.1) | copy-start | bytes 393220
  15.9 9.8 %copy-start.12 = (bf16[2,128,256]{1,2,0:T(8,128)(2,1)}, bf16[2,128,256]{1,2,0:T(8,128)(2,1)S(1)}, u32[]{:S(2)}) copy-start(bf16[2,128,256]{1,2,0:T(8,128)(2,1)S(1)} %collective-permute-done) | copy-start | bytes 393220
  16.0 12.6 %collective-permute-start.2 = (bf16[2,384,128]{1,2,0:T(8,128)(2,1)S(1)}, bf16[2,384,128]{1,2,0:T(8,128)(2,1)S(1)}, u32[]{:S(2)}, u32[]{:S(2)}) collective-permute-start(bf16[2,384,128]{1,2,0:T(8,128)(2,1)S(1)} %get-tuple-element.547), channel_id=1, source_target_pairs={{0,4},{4,8},{8,12},{12,16},{16,20},{20,24},{24,28},{1,5},{5,9},{9,... | collective-permute-start | bytes 589832 | tf_op jit(solution)/shard_map/ppermute | solution.py:16
  23.7 15.9 %collective-permute-start.3 = (bf16[2,384,128]{1,2,0:T(8,128)(2,1)S(1)}, bf16[2,384,128]{1,2,0:T(8,128)(2,1)}, u32[]{:S(2)}, u32[]{:S(2)}) collective-permute-start(bf16[2,384,128]{1,2,0:T(8,128)(2,1)S(1)} %get-tuple-element.548), channel_id=1, source_target_pairs={{4,0},{8,4},{12,8},{16,12},{20,16},{24,20},{28,24},{5,1},{9,5},{13... | collective-permute-start | bytes 589832 | tf_op jit(solution)/shard_map/ppermute | solution.py:19
  25.7 0.8 copy-start.1
  25.7 16.7 %copy-start.3 = (f32[2,256,256]{2,1,0:T(8,128)}, f32[2,256,256]{2,1,0:T(8,128)S(1)}, u32[]{:S(2)}) copy-start(f32[2,256,256]{2,1,0:T(8,128)S(1)} %get-tuple-element.762) | copy-start | bytes 1572868
  25.8 13.8 %copy-start.11 = (bf16[2,128,256]{1,2,0:T(8,128)(2,1)S(1)}, bf16[2,128,256]{1,2,0:T(8,128)(2,1)}, u32[]{:S(2)}) copy-start(bf16[2,128,256]{1,2,0:T(8,128)(2,1)} %copy-done.10) | copy-start | bytes 393220
  25.8 13.8 %copy-start.13 = (bf16[2,128,256]{1,2,0:T(8,128)(2,1)S(1)}, bf16[2,128,256]{1,2,0:T(8,128)(2,1)}, u32[]{:S(2)}) copy-start(bf16[2,128,256]{1,2,0:T(8,128)(2,1)} %copy-done.12) | copy-start | bytes 393220
  40.7 3.3 %copy-start.15 = (s32[1,1,2,2]{3,2,1,0:T(2,128)S(1)}, s32[1,1,2,2]{3,2,1,0:T(2,128)}, u32[]{:S(2)}) copy-start(s32[1,1,2,2]{3,2,1,0:T(2,128)} %param.24) | copy-start | bytes 52
  153.0 4.5 %copy-start.5 = (f32[1,1,2,256,256]{3,4,2,1,0:T(8,128)S(1)}, f32[1,1,2,256,256]{3,4,2,1,0:T(8,128)}, u32[]{:S(2)}) copy-start(f32[1,1,2,256,256]{3,4,2,1,0:T(8,128)} %copy.61) | copy-start | bytes 1572868 | tf_op jit(solution)/shard_map/while
  153.0 4.5 %copy-start.7 = (f32[256,256]{0,1:T(8,128)S(1)}, f32[256,256]{0,1:T(8,128)}, u32[]{:S(2)}) copy-start(f32[256,256]{0,1:T(8,128)} %fusion.264) | copy-start | bytes 786436 | tf_op jit(solution)/shard_map/while
  158.7 3.6 %copy-start.6 = (bf16[1,1,2,256,256]{4,3,2,1,0:T(8,128)(2,1)S(1)}, bf16[1,1,2,256,256]{4,3,2,1,0:T(8,128)(2,1)}, u32[]{:S(2)}) copy-start(bf16[1,1,2,256,256]{4,3,2,1,0:T(8,128)(2,1)} %copy.64) | copy-start | bytes 786436 | tf_op jit(solution)/shard_map/while
  161.1 2.4 copy-start
  161.1 2.4 copy-start.2
  161.1 2.4 copy-start.4
  178.5 9.1 %collective-permute-start.4 = (bf16[3,128,512]{2,1,0:T(8,128)(2,1)S(1)}, bf16[3,128,512]{2,1,0:T(8,128)(2,1)S(1)}, u32[]{:S(2)}, u32[]{:S(2)}) collective-permute-start(bf16[3,128,512]{2,1,0:T(8,128)(2,1)S(1)} %get-tuple-element.541), channel_id=1, source_target_pairs={{0,32},{32,64},{64,96},{96,128},{128,160},{160,192},{192,224},{224... | collective-permute-start | bytes 1179656 | tf_op jit(solution)/shard_map/ppermute | solution.py:16
  180.4 44.7 %collective-permute-start.5 = (bf16[3,128,512]{2,1,0:T(8,128)(2,1)S(1)}, bf16[3,128,512]{2,1,0:T(8,128)(2,1)S(1)}, u32[]{:S(2)}, u32[]{:S(2)}) collective-permute-start(bf16[3,128,512]{2,1,0:T(8,128)(2,1)S(1)} %get-tuple-element.542), channel_id=1, source_target_pairs={{32,0},{64,32},{96,64},{128,96},{160,128},{192,160},{224,192},{256... | collective-permute-start | bytes 1179656 | tf_op jit(solution)/shard_map/ppermute | solution.py:19
  225.4 8.5 %collective-permute-start.6 = (bf16[3,128,128]{2,1,0:T(8,128)(2,1)S(1)}, bf16[3,128,128]{2,1,0:T(8,128)(2,1)S(1)}, u32[]{:S(2)}, u32[]{:S(2)}) collective-permute-start(bf16[3,128,128]{2,1,0:T(8,128)(2,1)S(1)} %get-tuple-element.545), channel_id=1, source_target_pairs={{0,4},{4,8},{8,12},{12,16},{16,20},{20,24},{24,28},{1,5},{5,9},{9,... | collective-permute-start | bytes 294920 | tf_op jit(solution)/shard_map/ppermute | solution.py:16
  231.7 12.5 %collective-permute-start.7 = (bf16[3,128,128]{2,1,0:T(8,128)(2,1)S(1)}, bf16[3,128,128]{2,1,0:T(8,128)(2,1)S(1)}, u32[]{:S(2)}, u32[]{:S(2)}) collective-permute-start(bf16[3,128,128]{2,1,0:T(8,128)(2,1)S(1)} %get-tuple-element.546), channel_id=1, source_target_pairs={{4,0},{8,4},{12,8},{16,12},{20,16},{24,20},{28,24},{5,1},{9,5},{13... | collective-permute-start | bytes 294920 | tf_op jit(solution)/shard_map/ppermute | solution.py:19
  244.3 21.3 %copy-start.9 = (f32[2,128,256]{2,1,0:T(8,128)S(1)}, f32[2,128,256]{2,1,0:T(8,128)}, u32[]{:S(2)}) copy-start(f32[2,128,256]{2,1,0:T(8,128)} %param.21) | copy-start | bytes 786436
  (1 other events, 0.7 us)
Sparse Core Ops, SparseCore 0:
  64.1 73.4 all-reduce.1
